TPU v7x, 32 devices: a whole 2x2x4 slice. The times are simulated.
32 devices in a mesh: prow: 4 (over z), pcol: 8 (over y, x, core).
Axes of the slice: x: 2, y: 2, z: 4, core: 2. Of those that a mesh axis runs over, the one named last changes fastest.
Arguments:
- matrix: float32 [2, 4, 256, 8, 256], P(None, 'prow', None, 'pcol'), may hold values from -6 to 6, as said below
Outputs:
- factored: float32 [2, 4, 256, 8, 256], P(None, 'prow', None, 'pcol')
Inputs may be any that keep to these rules, and one draw needn't show every extreme that they name: `matrix`: in the first 3 diagonal blocks every diagonal entry lies between 1.3 and 3.2, and diag(1/d) times the off-diagonal part of each such block has spectral norm below about 0.7.
All inputs are finite; a program needn't handle non-finite values.
Results may differ from a plain program's by a relative error of at most 0.0001.
Values sent between devices are 32-bit elements; how exact they have to be, the bound alone decides.
No kernel may reach another device: no remote copies, remote signals or barrier semaphores. Data moves between devices by JAX's collectives and lax.ppermute only.
A program may use at most 64 MiB of HBM per device.

v0:
```python
import jax
import jax.numpy as jnp
from jax import lax
from jax.sharding import PartitionSpec as P

PANELS = 3


def from_root(block, axis, owner):
    block = jnp.where(lax.axis_index(axis) == owner, block, jnp.zeros_like(block))
    return lax.psum(block, axis)


def invert(block):
    scales = 1.0 / jnp.diagonal(block)
    first = 2.0 * jnp.diag(scales) - scales[:, None] * block * scales[None, :]
    inner = jnp.dot(block, first, precision=lax.Precision.HIGHEST)
    return 2.0 * first - jnp.dot(first, inner, precision=lax.Precision.HIGHEST)


def blockwise(left, right):
    return jnp.einsum("rij,jk->rik", left, right, precision=lax.Precision.HIGHEST)


def empty_like(block):
    return jnp.zeros_like(block)


def body(matrix):
    shape = matrix.shape
    tile = matrix.reshape(shape[0], shape[2], shape[4])
    my_row = lax.axis_index("prow")
    my_col = lax.axis_index("pcol")
    row_count = lax.axis_size("prow")
    block_row = (jnp.arange(shape[0], dtype=jnp.int32) * row_count + my_row)[:, None, None]
    for panel in range(PANELS):
        below = block_row > panel
        owns_pivot = (my_row == panel) & (my_col == panel)
        local_inverse = lax.cond(owns_pivot, invert, empty_like, tile[0])
        inverse = from_root(local_inverse, "prow", panel)

        def make_factors(operands):
            return jnp.where(below, blockwise(operands[0], operands[1]), 0.0)

        def no_factors(operands):
            return jnp.zeros_like(operands[0])

        local_factors = lax.cond(my_col == panel, make_factors, no_factors, (tile, inverse))
        factors = from_root(local_factors, "pcol", panel)
        pivot_row = from_root(tile[0], "prow", panel)
        update = blockwise(factors, pivot_row)
        tile = jnp.where(below & (my_col > panel), tile - update, tile)
        column = jnp.where(below, factors, jnp.where(block_row == panel, inverse[None], tile))
        tile = jnp.where(my_col == panel, column, tile)
    return tile.reshape(shape)


def solution(mesh):
    return jax.shard_map(
        body,
        mesh=mesh,
        in_specs=(P(None, "prow", None, "pcol", None),),
        out_specs=P(None, "prow", None, "pcol", None),
        check_vma=False,
    )
```

profile of v0, /device:TPU:0, one launch (start us, length us, event | category | flops | bytes accessed | tf_op | source)
XLA Modules:
  0.0 320.0 jit_solution(9454973679262351808)
XLA Ops:
  6.5 1.1 slice.13
  7.7 3.5 %conditional.6 = (f32[256,256]{1,0:T(8,128)S(1)}) conditional(s32[]{:T(128)} %convert_element_type.21, () %tuple.44, f32[256,256]{1,0:T(8,128)S(1)} %bitcast.62), branch_computations={%region_0.0_spmd, %region_1.2_spmd} | conditional | flops 403965184 | bytes 1319944 | solution.py:39
  7.7 2.3 gather_fusion
  10.1 0.7 fusion.3
  10.8 0.4 convolution_subtract_fusion
  11.2 0.8 broadcast_select_fusion.7
  12.1 0.0 all-reduce.10.cloned.1.call-start
  12.1 1.0 copy-done
  13.1 38.1 %all-reduce.20.cloned.1.call-done = (f32[256,256]{1,0:T(8,128)}, f32[256,256]{1,0:T(8,128)}) async-done(((f32[256,256]{1,0:T(8,128)}, f32[256,256]{1,0:T(8,128)}), (f32[256,256]{1,0:T(8,128)}, f32[256,256]{1,0:T(8,128)})) %all-reduce.20.cloned.1.call-update) | async-done | bytes 524304 | tf_op jit(solution)/shard_map/psum | solution.py:11
  51.2 1.5 conditional.7
  51.2 1.5 convolution_select_fusion
  52.8 0.8 broadcast_select_fusion.2
  53.6 0.0 all-reduce.10.cloned.1.call-update
  53.6 0.0 all-reduce.18.cloned.1.call-start
  53.7 55.3 %all-reduce.10.cloned.1.call-done = f32[2,256,256]{2,1,0:T(8,128)} async-done(((f32[2,256,256]{2,1,0:T(8,128)}), f32[2,256,256]{2,1,0:T(8,128)}) %all-reduce.10.cloned.1.call-update) | async-done | bytes 524304 | tf_op jit(solution)/shard_map/psum | solution.py:11
  109.0 1.8 select_select_fusion.1
  110.9 0.7 broadcast_select_fusion.5
  111.6 0.7 broadcast_select_fusion.6
  112.4 0.0 all-reduce.12.cloned.1.call-start
  112.4 38.2 %all-reduce.18.cloned.1.call-done = (f32[256,256]{1,0:T(8,128)}, f32[256,256]{1,0:T(8,128)}) async-done(((f32[256,256]{1,0:T(8,128)}, f32[256,256]{1,0:T(8,128)}), (f32[256,256]{1,0:T(8,128)}, f32[256,256]{1,0:T(8,128)})) %all-reduce.18.cloned.1.call-update) | async-done | bytes 524304 | tf_op jit(solution)/shard_map/psum | solution.py:11
  150.7 0.8 broadcast_select_fusion.1
  151.6 0.0 all-reduce.16.cloned.1.call-start
  151.7 56.6 %all-reduce.12.cloned.1.call-done = f32[2,256,256]{2,1,0:T(8,128)} async-done(((f32[2,256,256]{2,1,0:T(8,128)}), f32[2,256,256]{2,1,0:T(8,128)}) %all-reduce.12.cloned.1.call-update) | async-done | bytes 524304 | tf_op jit(solution)/shard_map/psum | solution.py:11
  208.3 1.8 select_select_fusion
  210.2 0.7 broadcast_select_fusion.3
  210.9 0.7 broadcast_select_fusion.4
  211.7 0.0 all-reduce.14.cloned.1.call-start
  211.7 40.6 %all-reduce.16.cloned.1.call-done = (f32[256,256]{1,0:T(8,128)}, f32[256,256]{1,0:T(8,128)}) async-done(((f32[256,256]{1,0:T(8,128)}, f32[256,256]{1,0:T(8,128)}), (f32[256,256]{1,0:T(8,128)}, f32[256,256]{1,0:T(8,128)})) %all-reduce.16.cloned.1.call-update) | async-done | bytes 524304 | tf_op jit(solution)/shard_map/psum | solution.py:11
  252.4 0.8 broadcast_select_fusion
  253.3 56.7 %all-reduce.14.cloned.1.call-done = f32[2,256,256]{2,1,0:T(8,128)} async-done(((f32[2,256,256]{2,1,0:T(8,128)}), f32[2,256,256]{2,1,0:T(8,128)}) %all-reduce.14.cloned.1.call-update) | async-done | bytes 524304 | tf_op jit(solution)/shard_map/psum | solution.py:11
  310.0 1.8 select_bitcast_fusion
  311.8 1.3 copy.5
  (41 shorter events, 0.5 us)
Async XLA Ops:
  6.5 44.7 %all-reduce.20.cloned.1.call-start = ((), (), s32[]{:S(2)}) async-start(), calls=%async_computation.5 | async-start | bytes 1048576 | tf_op jit(solution)/shard_map/psum | solution.py:11
  12.0 1.0 copy-start
  12.1 96.9 %all-reduce.10.cloned.1.call-start = ((), (), s32[]{:S(2)}) async-start(), calls=%async_computation | async-start | bytes 1048576 | tf_op jit(solution)/shard_map/psum | solution.py:11
  53.6 55.4 %copy-start.1 = (f32[256,256]{1,0:T(8,128)S(1)}, f32[256,256]{1,0:T(8,128)}, u32[]{:S(2)}) copy-start(f32[256,256]{1,0:T(8,128)} %get-tuple-element.66) | copy-start | bytes 786436
  53.6 55.4 %copy-start.4 = (f32[256,256]{1,0:T(8,128)S(1)}, f32[256,256]{1,0:T(8,128)}, u32[]{:S(2)}) copy-start(f32[256,256]{1,0:T(8,128)} %get-tuple-element.67) | copy-start | bytes 786436
  53.6 97.0 %all-reduce.18.cloned.1.call-start = ((), (), s32[]{:S(2)}) async-start(), calls=%async_computation.4 | async-start | bytes 1048576 | tf_op jit(solution)/shard_map/psum | solution.py:11
  112.4 95.9 %all-reduce.12.cloned.1.call-start = ((), (), s32[]{:S(2)}) async-start(), calls=%async_computation.1 | async-start | bytes 1048576 | tf_op jit(solution)/shard_map/psum | solution.py:11
  151.6 56.8 %copy-start.2 = (f32[256,256]{1,0:T(8,128)S(1)}, f32[256,256]{1,0:T(8,128)}, u32[]{:S(2)}) copy-start(f32[256,256]{1,0:T(8,128)} %get-tuple-element.64) | copy-start | bytes 786436
  151.6 56.8 %copy-start.5 = (f32[256,256]{1,0:T(8,128)S(1)}, f32[256,256]{1,0:T(8,128)}, u32[]{:S(2)}) copy-start(f32[256,256]{1,0:T(8,128)} %get-tuple-element.65) | copy-start | bytes 786436
  151.6 100.7 %all-reduce.16.cloned.1.call-start = ((), (), s32[]{:S(2)}) async-start(), calls=%async_computation.3 | async-start | bytes 1048576 | tf_op jit(solution)/shard_map/psum | solution.py:11
  211.7 98.3 %all-reduce.14.cloned.1.call-start = ((), (), s32[]{:S(2)}) async-start(), calls=%async_computation.2 | async-start | bytes 1048576 | tf_op jit(solution)/shard_map/psum | solution.py:11
  253.2 56.8 %copy-start.3 = (f32[256,256]{1,0:T(8,128)S(1)}, f32[256,256]{1,0:T(8,128)}, u32[]{:S(2)}) copy-start(f32[256,256]{1,0:T(8,128)} %get-tuple-element.62) | copy-start | bytes 786436
  253.2 56.8 %copy-start.6 = (f32[256,256]{1,0:T(8,128)S(1)}, f32[256,256]{1,0:T(8,128)}, u32[]{:S(2)}) copy-start(f32[256,256]{1,0:T(8,128)} %get-tuple-element.63) | copy-start | bytes 786436
Sparse Core Ops, SparseCore 0:
  12.2 39.0 all-reduce.19
  54.3 54.6 all-reduce.9
  112.5 38.1 all-reduce.17
  153.6 54.6 all-reduce.11
  211.8 40.4 all-reduce.15
  255.3 54.6 all-reduce.13
where the time goes:
time: 320 us
  waiting for transfers between devices  286 us (89%)
  between operations  13.7 us (4%)
  matrix products  8.1 us (3%)
  other arithmetic  6.29 us (2%)
  local copies, waits for them, and re-layouts  5.99 us (2%)
    psum x6, waiting for transfers between devices, from_root(): return lax.psum(block, axis)  286 us
    dot_general x4, matrix products, blockwise(): jnp.einsum('rij,jk->rik', left, right, precision=lax.Precision.HIGHEST)  7.01 us
  transfers between devices with their start and end apart: 6, of which 6 were waited for; matrix products, arithmetic and copies ran while one was open for 0% of the time, Pallas kernels for 0%

commit v1 on v0

--- a/solution.py
+++ b/solution.py
@@ -8,7 +8,7 @@
 
 def from_root(block, axis, owner):
     block = jnp.where(lax.axis_index(axis) == owner, block, jnp.zeros_like(block))
-    return lax.psum(block, axis)
+    return jnp.sum(lax.all_gather(block, axis), axis=0)
 
 
 def invert(block):

time: 320 us -> 321 us (level)
  other arithmetic: 6.29 us -> 22.5 us
  waiting for transfers between devices: 286 us -> 275 us
  matrix products: 8.1 us -> 3.49 us
    psum x6 -> x0, waiting for transfers between devices: 286 us -> none  [from_root(): return lax.psum(block, axis)]
    all_gather x0 -> x9, waiting for transfers between devices: none -> 273 us  [from_root(): return jnp.sum(lax.all_gather(block, axis), axis=0)]
    reduce_sum x0 -> x9, other arithmetic: none -> 15.5 us  [from_root(): return jnp.sum(lax.all_gather(block, axis), axis=0)]
    dot_general x4, matrix products: 7.01 us -> 2.39 us  [blockwise(): jnp.einsum('rij,jk->rik', left, right, precision=lax.Precision.HIGHEST)]
    select_n x8 -> x9, other arithmetic: 6.22 us -> 6.93 us  [from_root(): jnp.where(lax.axis_index(axis) == owner, block, jnp.zeros_like(block))]
  transfers between devices with their start and end apart: 6 -> 9, of which waited for: 6 -> 9; matrix products, arithmetic and copies ran while one was open for 0% -> 3% of each run, Pallas kernels for 0% -> 0%
where the time goes in v1:
time: 321 us; the launch traced here: 320 us
  waiting for transfers between devices  275 us (86%)
  other arithmetic  22.5 us (7%)
  between operations  13.4 us (4%)
  local copies, waits for them, and re-layouts  5.02 us (2%)
  matrix products  3.49 us (1%)
    all_gather x9, waiting for transfers between devices, from_root(): return jnp.sum(lax.all_gather(block, axis), axis=0)  273 us
    reduce_sum x9, other arithmetic, from_root(): return jnp.sum(lax.all_gather(block, axis), axis=0)  15.5 us
    select_n x9, other arithmetic, from_root(): jnp.where(lax.axis_index(axis) == owner, block, jnp.zeros_like(block))  6.93 us
  transfers between devices with their start and end apart: 9, of which 9 were waited for; matrix products, arithmetic and copies ran while one was open for 3% of the time, Pallas kernels for 0%

profile of v1, /device:TPU:0, one launch (start us, length us, event | category | flops | bytes accessed | tf_op | source)
XLA Modules:
  0.0 320.1 jit_solution(6720201952212407323)
XLA Ops:
  6.5 1.2 slice.16
  7.7 0.8 broadcast_select_fusion.5
  8.5 3.5 %conditional.6 = (f32[256,256]{1,0:T(8,128)S(1)}) conditional(s32[]{:T(128)} %convert_element_type.21, () %tuple.44, f32[1,1,256,1,256]{4,2,3,1,0:T(8,128)S(1)} %get-tuple-element.70), branch_computations={%region_0.0_spmd, %region_1.2_spmd} | conditional | flops 403965184 | bytes 1319944 | solution.py:39
  8.5 2.3 gather_fusion
  12.0 0.7 broadcast_select_fusion.8
  12.8 0.7 all-gather.25.cloned.1.call-update
  13.6 26.5 %all-gather.21.cloned.1.call-done = f32[1024,256]{1,0:T(8,128)} async-done(((f32[256,256]{1,0:T(8,128)}), f32[1024,256]{1,0:T(8,128)}) %all-gather.21.cloned.1.call-update) | async-done | bytes 1048592 | tf_op jit(solution)/shard_map/all_gather | solution.py:11
  40.1 1.3 reduce_sum.81
  42.1 0.8 broadcast_select_fusion.2
  43.0 26.1 %all-gather.25.cloned.1.call-done = f32[4,1,256,1,256]{4,2,3,1,0:T(8,128)} async-done(((f32[1,1,256,1,256]{4,2,3,1,0:T(8,128)}), f32[4,1,256,1,256]{4,2,3,1,0:T(8,128)}) %all-gather.25.cloned.1.call-update) | async-done | bytes 1048592 | tf_op jit(solution)/shard_map/all_gather | solution.py:11
  69.1 1.3 reduce_sum.83
  70.4 36.6 %all-gather.23.cloned.1.call-done = f32[16,256,256]{2,1,0:T(8,128)} async-done(((f32[2,256,256]{2,1,0:T(8,128)}), f32[16,256,256]{2,1,0:T(8,128)}) %all-gather.23.cloned.1.call-update) | async-done | bytes 4194320 | tf_op jit(solution)/shard_map/all_gather | solution.py:11
  107.0 2.5 reduce_sum.82
  110.1 0.8 broadcast_select_fusion.4
  110.9 0.7 broadcast_select_fusion.7
  112.3 28.1 %all-gather.27.cloned.1.call-done = f32[1024,256]{1,0:T(8,128)} async-done(((f32[256,256]{1,0:T(8,128)}), f32[1024,256]{1,0:T(8,128)}) %all-gather.27.cloned.1.call-update) | async-done | bytes 1048592 | tf_op jit(solution)/shard_map/all_gather | solution.py:11
  140.4 1.3 reduce_sum.84
  141.8 0.8 broadcast_select_fusion.1
  142.7 26.5 %all-gather.17.cloned.1.call-done = f32[4,256,256]{2,1,0:T(8,128)} async-done(((f32[1,256,256]{2,1,0:T(8,128)}), f32[4,256,256]{2,1,0:T(8,128)}) %all-gather.17.cloned.1.call-update) | async-done | bytes 1048592 | tf_op jit(solution)/shard_map/all_gather | solution.py:11
  169.2 1.3 reduce_sum.86
  170.5 36.4 %all-gather.29.cloned.1.call-done = f32[16,256,256]{2,1,0:T(8,128)} async-done(((f32[2,256,256]{2,1,0:T(8,128)}), f32[16,256,256]{2,1,0:T(8,128)}) %all-gather.29.cloned.1.call-update) | async-done | bytes 4194320 | tf_op jit(solution)/shard_map/all_gather | solution.py:11
  206.9 2.5 reduce_sum.85
  210.1 0.8 broadcast_select_fusion.3
  210.8 0.7 broadcast_select_fusion.6
  212.4 29.9 %all-gather.31.cloned.1.call-done = f32[1024,256]{1,0:T(8,128)} async-done(((f32[256,256]{1,0:T(8,128)}), f32[1024,256]{1,0:T(8,128)}) %all-gather.31.cloned.1.call-update) | async-done | bytes 1048592 | tf_op jit(solution)/shard_map/all_gather | solution.py:11
  242.3 1.3 reduce_sum.87
  243.6 0.8 broadcast_select_fusion
  244.5 26.7 %all-gather.19.cloned.1.call-done = f32[4,256,256]{2,1,0:T(8,128)} async-done(((f32[1,256,256]{2,1,0:T(8,128)}), f32[4,256,256]{2,1,0:T(8,128)}) %all-gather.19.cloned.1.call-update) | async-done | bytes 1048592 | tf_op jit(solution)/shard_map/all_gather | solution.py:11
  271.2 1.3 reduce_sum.89
  272.5 36.6 %all-gather.33.cloned.1.call-done = f32[16,256,256]{2,1,0:T(8,128)} async-done(((f32[2,256,256]{2,1,0:T(8,128)}), f32[16,256,256]{2,1,0:T(8,128)}) %all-gather.33.cloned.1.call-update) | async-done | bytes 4194320 | tf_op jit(solution)/shard_map/all_gather | solution.py:11
  309.1 2.5 reduce_sum.88
  312.2 1.3 copy.7
  (45 shorter events, 6.1 us)
Async XLA Ops:
  6.5 7.0 %copy-start = (f32[2,1,256,1,256]{4,3,2,1,0:T(1,128)S(1)}, f32[2,1,256,1,256]{4,3,2,1,0:T(1,128)}, u32[]{:S(2)}) copy-start(f32[2,1,256,1,256]{4,3,2,1,0:T(1,128)} %param.13) | copy-start | bytes 1572868
  6.5 33.6 %all-gather.21.cloned.1.call-start = ((), (), s32[]{:S(2)}) async-start(), calls=%async_computation.2 | async-start | bytes 1310720 | tf_op jit(solution)/shard_map/all_gather | solution.py:11
  12.7 56.4 %all-gather.25.cloned.1.call-start = ((), (), s32[]{:S(2)}) async-start(), calls=%async_computation.4 | async-start | bytes 1310720 | tf_op jit(solution)/shard_map/all_gather | solution.py:11
  13.5 93.5 %all-gather.23.cloned.1.call-start = ((), (), s32[]{:S(2)}) async-start(), calls=%async_computation.3 | async-start | bytes 4718592 | tf_op jit(solution)/shard_map/all_gather | solution.py:11
  42.9 97.4 %all-gather.27.cloned.1.call-start = ((), (), s32[]{:S(2)}) async-start(), calls=%async_computation.5 | async-start | bytes 1310720 | tf_op jit(solution)/shard_map/all_gather | solution.py:11
  111.7 57.5 %all-gather.17.cloned.1.call-start = ((), (), s32[]{:S(2)}) async-start(), calls=%async_computation | async-start | bytes 1310720 | tf_op jit(solution)/shard_map/all_gather | solution.py:11
  112.2 94.7 %all-gather.29.cloned.1.call-start = ((), (), s32[]{:S(2)}) async-start(), calls=%async_computation.6 | async-start | bytes 4718592 | tf_op jit(solution)/shard_map/all_gather | solution.py:11
  142.6 99.6 %all-gather.31.cloned.1.call-start = ((), (), s32[]{:S(2)}) async-start(), calls=%async_computation.7 | async-start | bytes 1310720 | tf_op jit(solution)/shard_map/all_gather | solution.py:11
  211.6 59.6 %all-gather.19.cloned.1.call-start = ((), (), s32[]{:S(2)}) async-start(), calls=%async_computation.1 | async-start | bytes 1310720 | tf_op jit(solution)/shard_map/all_gather | solution.py:11
  212.3 96.8 %all-gather.33.cloned.1.call-start = ((), (), s32[]{:S(2)}) async-start(), calls=%async_computation.8 | async-start | bytes 4718592 | tf_op jit(solution)/shard_map/all_gather | solution.py:11
Sparse Core Ops, SparseCore 0:
  12.8 27.2 all-gather.20
  41.7 27.3 all-gather.24
  71.0 35.9 all-gather.22
  111.8 28.5 all-gather.26
  141.8 27.3 all-gather.16
  170.9 35.9 all-gather.28
  211.7 30.4 all-gather.30
  243.8 27.3 all-gather.18
  273.1 35.9 all-gather.32
